TPU v7x, 256 devices: a whole 4x4x8 slice. The times are simulated.
256 devices in a mesh: grp: 4 (over y), wide: 64 (over z, x, core).
Axes of the slice: x: 4, y: 4, z: 8, core: 2. Of those that a mesh axis runs over, the one named last changes fastest.
Arguments:
- tiles: bfloat16 [12288, 256, 256], P(('grp', 'wide')), may hold values from -0.59765625 to 0.59765625
- contraction: int32 [12288], P(('grp', 'wide')), may hold values from 0 to 15
- row_tile: int32 [12288], P(('grp', 'wide')), may hold values from 0 to 255, as said below
- owner_map: int32 [256], replicated, may hold values from 0 to 255, as said below
- panel: bfloat16 [4096, 768], P('grp'), may hold values from -0.5390625 to 0.5390625
Outputs:
- column_block: float32 [65536, 768], P('wide')
Inputs may be any that keep to these rules, and one draw needn't show every extreme that they name: `row_tile`: every row tile's owner is owner_map // 4; among the 48 contributions of one device at most 2 have row tiles of one owner, and on every device some owner gets exactly 2. `owner_map`: A permutation of the row tiles.
All inputs are finite; a program needn't handle non-finite values.
Results may differ from a plain program's by a relative error of at most 0.0003.
Values may be sent and summed in bfloat16 or wider, within the bound.
A program may use at most 192 MiB of HBM per device.

v0:
```python
import math
import jax
import jax.numpy as jnp
from jax import lax
from jax.sharding import PartitionSpec as P


def place_slots(row_ids, owner_map, out_dev):
    table_ids = jnp.arange(owner_map.shape[0], dtype=jnp.int32)
    position = jnp.sum(jnp.where(row_ids[..., None] == table_ids, owner_map, 0), axis=-1)
    target = position // out_dev
    serial = jnp.arange(row_ids.shape[-1], dtype=jnp.int32)
    earlier = (target[..., :, None] == target[..., None, :]) & (serial[:, None] > serial[None, :])
    ranking = jnp.sum(earlier.astype(jnp.int32), axis=-1)
    return (position % out_dev, target, ranking)


def add_products(summed, arrived, slot_labels, panel_tiles):
    slot_count = arrived.shape[0]
    block_rows = math.gcd(slot_count, 32)
    out_dev = summed.shape[0]
    local_ids = jnp.arange(out_dev, dtype=jnp.int32)

    def one_block(which_block, running, source_tiles, source_labels):
        part_tiles = lax.dynamic_slice_in_dim(source_tiles, which_block * block_rows, block_rows, 0)
        part_labels = lax.dynamic_slice_in_dim(
            source_labels, which_block * block_rows, block_rows, 0
        )
        chosen = jnp.take(panel_tiles, part_labels[:, 1], axis=0)
        products = jnp.einsum(
            "sab,sbc->sac", part_tiles, chosen, preferred_element_type=jnp.float32
        )
        row_hits = (part_labels[:, 0][:, None] == local_ids[None, :]).astype(jnp.float32)
        return running + jnp.einsum(
            "sr,sac->rac", row_hits, products, precision=lax.Precision.HIGHEST
        )

    return lax.fori_loop(
        0,
        slot_count // block_rows,
        lambda which_block, running: one_block(which_block, running, arrived, slot_labels),
        summed,
    )


def per_device(tiles, contraction, row_tile, owner_map, panel):
    wide_count = lax.axis_size("wide")
    tile_dev = tiles.shape[0]
    tile_side = tiles.shape[1]
    out_dev = owner_map.shape[0] // wide_count
    most_slots = tile_dev * 8 // (3 * wide_count)
    slot_total = wide_count * most_slots
    local_row, target, ranking = place_slots(row_tile, owner_map, out_dev)
    slot_index = target * most_slots + ranking
    outgoing = jnp.zeros((slot_total, tile_side, tile_side), tiles.dtype).at[slot_index].set(tiles)
    all_rows, all_contraction = (
        lax.all_gather(row_tile, "wide", axis=0, tiled=True),
        lax.all_gather(contraction, "wide", axis=0, tiled=True),
    )
    all_rows = all_rows.reshape(wide_count, tile_dev)
    all_contraction = all_contraction.reshape(wide_count, tile_dev)
    source_local, source_target, source_rank = place_slots(all_rows, owner_map, out_dev)
    source_ids = jnp.arange(wide_count, dtype=jnp.int32)
    mine = source_target == lax.axis_index("wide")
    arrive_index = jnp.where(mine, source_ids[:, None] * most_slots + source_rank, slot_total)
    label_pairs = jnp.stack([source_local, all_contraction], axis=-1).reshape(
        wide_count * tile_dev, 2
    )
    vacant_label = jnp.stack(
        [jnp.full((slot_total,), out_dev, jnp.int32), jnp.zeros((slot_total,), jnp.int32)], axis=1
    )
    arrived_labels = vacant_label.at[arrive_index.reshape(-1)].set(label_pairs, mode="drop")
    gathered = lax.all_gather(panel, "grp", axis=0, tiled=True)
    panel_tiles = gathered.reshape(gathered.shape[0] // tile_side, tile_side, gathered.shape[1])
    summed = jnp.zeros((out_dev, tile_side, gathered.shape[1]), jnp.float32)
    arrived = lax.all_to_all(outgoing, "wide", split_axis=0, concat_axis=0, tiled=True)
    summed = add_products(summed, arrived, arrived_labels, panel_tiles)
    summed = lax.psum(summed, "grp")
    return summed.reshape(out_dev * tile_side, gathered.shape[1])


def solution(mesh):
    return jax.shard_map(
        per_device,
        mesh=mesh,
        in_specs=(
            P(("grp", "wide"), None, None),
            P(("grp", "wide")),
            P(("grp", "wide")),
            P(),
            P("grp", None),
        ),
        out_specs=P("wide", None),
        check_vma=False,
    )
```

profile of v0, /device:TPU:1, one launch (start us, length us, event | category | flops | bytes accessed | tf_op | source)
XLA Modules:
  0.0 973.6 jit_solution(2914574177467141061)
XLA Ops:
  6.5 0.9 select_reduce_fusion.1
  7.4 0.2 convert_reduce_fusion.1
  7.6 5.9 broadcast_in_dim.68
  13.5 16.8 %scatter_fusion.1 = bf16[128,256,256]{2,1,0:T(8,128)(2,1)} fusion(bf16[128,256,256]{2,1,0:T(8,128)(2,1)} %broadcast_in_dim.68, s32[48]{0:T(128)S(1)} %fusion.19, bf16[48,256,256]{2,1,0:T(8,128)(2,1)} %param.7), kind=kCustom, calls=%fused_computation.2 | custom fusion | bytes 18874560 | tf_op jit(solution)/shard_map/scatter | solution.py:55
  30.4 0.0 copy-start.4
  30.4 0.0 copy-start.2
  30.4 0.0 copy-start.3
  30.4 0.0 copy-start.1
  30.4 13.3 %all-to-all-start = ((bf16[128,256,256]{2,1,0:T(8,128)(2,1)}), bf16[128,256,256]{2,1,0:T(8,128)(2,1)}, u32[]{:S(2)}, u32[]{:S(2)}) async-start(bf16[128,256,256]{2,1,0:T(8,128)(2,1)} %scatter_fusion.1), calls=%async_computation | async-start | bytes 33554432 | tf_op jit(solution)/shard_map/all_to_all | solution.py:76
  43.6 0.0 copy-start
  43.6 0.0 all-gather.2.cloned.1.call-start
  43.7 0.7 all-gather.2.cloned.1.call-update
  44.4 0.0 all-reduce.5.cloned.1.call-start
  44.5 0.0 copy-done.4
  44.5 0.6 dynamic-slice
  45.7 0.0 copy-done.2
  45.7 0.3 dynamic-update-slice
  46.0 0.0 copy-done.3
  46.0 0.3 dynamic-update-slice.1
  46.3 588.5 %all-reduce.2 = (s32[3072]{0:T(1024)S(1)}, s32[3072]{0:T(1024)S(1)}) all-reduce(s32[3072]{0:T(1024)S(1)} %dynamic-update-slice, s32[3072]{0:T(1024)S(1)} %dynamic-update-slice.1), channel_id=1, replica_groups=mesh['grp'=4,'wide'=64] {'wide'}, use_global_device_ids=true, to_apply=%add | all-reduce | flops 6144 | bytes 49152
  634.8 0.1 eq.107
  634.9 0.0 copy-done.1
  634.9 1.7 select_reduce_fusion
  636.6 0.1 reduce_sum.43
  636.7 0.1 copy.11
  636.8 0.5 convert_reduce_fusion
  637.3 0.1 copy.13
  637.4 0.1 add.152
  637.5 0.1 and_select_fusion
  637.6 1.7 copy.14
  639.3 0.0 copy-done
  639.3 8.5 scatter_fusion
  647.8 0.1 copy.15
  647.9 0.0 all-gather.2.cloned.1.call-done
  647.9 0.0 all-to-all-done
  647.9 231.6 %while.14 = (s32[]{:T(128)}, f32[4,256,768]{2,0,1:T(4,128)S(1)}, s32[128,2]{0,1:T(2,128)S(1)}, bf16[128,256,256]{2,1,0:T(8,128)(2,1)}, bf16[16,256,768]{2,1,0:T(...) while((s32[]{:T(128)}, f32[4,256,768]{2,0,1:T(4,128)S(1)}, ...), condition=%wide.region_7.8_spmd.clone, body=%wide.region_6.7_spmd.clone.sunk | while | flops 3531081216 | bytes 98572000 | solution.py:38
  648.1 0.1 constant_dynamic-slice_fusion.2
  648.2 9.4 gather_fusion
  657.5 17.7 %fusion.29 = f32[32,256,768]{2,1,0:T(8,128)} fusion(bf16[32,256,768]{2,1,0:T(8,128)(2,1)} %gather_fusion, pred[32]{0:T(512)(128)(4,1)S(1)} %and_bitcast_fusion.2, bf16[128,256,256]{2,1,0:T(8,128)(2,1)} %get-tuple-element.217, s32[]{:T(128)S(6)} %select_n.171), kind=kOutput, calls=%fused_computation.6.clone.1 | convolution fusion | flops 3227516928 | bytes 41943076 | tf_op jit(solution)/shard_map/while/body/eval_jaxpr/sab,sbc->sac/dot_general | solution.py:30
  675.2 30.7 %select_add_fusion.2 = f32[4,256,768]{2,0,1:T(4,128)S(1)} fusion(f32[4,256,768]{2,0,1:T(4,128)S(1)} %get-tuple-element.206, pred[]{:T(512)S(6)} %compare.49, f32[32,256,768]{2,1,0:T(8,128)} %fusion.29, s32[32]{0:T(128)S(1)} %get-tuple-element.195), kind=kOutput, calls=%fused_computation.11.clone.1 | convolution fusion | flops 303562880 | bytes 31457408 | tf_op jit(solution)/shard_map/while/body/eval_jaxpr/sr,sac->rac/dot_general | solution.py:34
  706.0 0.1 constant_dynamic-slice_fusion.2
  706.1 9.3 gather_fusion
  715.4 17.7 %fusion.29 = f32[32,256,768]{2,1,0:T(8,128)} fusion(bf16[32,256,768]{2,1,0:T(8,128)(2,1)} %gather_fusion, pred[32]{0:T(512)(128)(4,1)S(1)} %and_bitcast_fusion.2, bf16[128,256,256]{2,1,0:T(8,128)(2,1)} %get-tuple-element.217, s32[]{:T(128)S(6)} %select_n.171), kind=kOutput, calls=%fused_computation.6.clone.1 | convolution fusion | flops 3227516928 | bytes 41943076 | tf_op jit(solution)/shard_map/while/body/eval_jaxpr/sab,sbc->sac/dot_general | solution.py:30
  733.1 30.7 %select_add_fusion.2 = f32[4,256,768]{2,0,1:T(4,128)S(1)} fusion(f32[4,256,768]{2,0,1:T(4,128)S(1)} %get-tuple-element.206, pred[]{:T(512)S(6)} %compare.49, f32[32,256,768]{2,1,0:T(8,128)} %fusion.29, s32[32]{0:T(128)S(1)} %get-tuple-element.195), kind=kOutput, calls=%fused_computation.11.clone.1 | convolution fusion | flops 303562880 | bytes 31457408 | tf_op jit(solution)/shard_map/while/body/eval_jaxpr/sr,sac->rac/dot_general | solution.py:34
  763.8 0.1 constant_dynamic-slice_fusion.2
  763.9 9.3 gather_fusion
  773.2 17.7 %fusion.29 = f32[32,256,768]{2,1,0:T(8,128)} fusion(bf16[32,256,768]{2,1,0:T(8,128)(2,1)} %gather_fusion, pred[32]{0:T(512)(128)(4,1)S(1)} %and_bitcast_fusion.2, bf16[128,256,256]{2,1,0:T(8,128)(2,1)} %get-tuple-element.217, s32[]{:T(128)S(6)} %select_n.171), kind=kOutput, calls=%fused_computation.6.clone.1 | convolution fusion | flops 3227516928 | bytes 41943076 | tf_op jit(solution)/shard_map/while/body/eval_jaxpr/sab,sbc->sac/dot_general | solution.py:30
  790.9 30.7 %select_add_fusion.2 = f32[4,256,768]{2,0,1:T(4,128)S(1)} fusion(f32[4,256,768]{2,0,1:T(4,128)S(1)} %get-tuple-element.206, pred[]{:T(512)S(6)} %compare.49, f32[32,256,768]{2,1,0:T(8,128)} %fusion.29, s32[32]{0:T(128)S(1)} %get-tuple-element.195), kind=kOutput, calls=%fused_computation.11.clone.1 | convolution fusion | flops 303562880 | bytes 31457408 | tf_op jit(solution)/shard_map/while/body/eval_jaxpr/sr,sac->rac/dot_general | solution.py:34
  821.7 0.1 constant_dynamic-slice_fusion.2
  821.8 9.2 gather_fusion
  831.0 17.7 %fusion.29 = f32[32,256,768]{2,1,0:T(8,128)} fusion(bf16[32,256,768]{2,1,0:T(8,128)(2,1)} %gather_fusion, pred[32]{0:T(512)(128)(4,1)S(1)} %and_bitcast_fusion.2, bf16[128,256,256]{2,1,0:T(8,128)(2,1)} %get-tuple-element.217, s32[]{:T(128)S(6)} %select_n.171), kind=kOutput, calls=%fused_computation.6.clone.1 | convolution fusion | flops 3227516928 | bytes 41943076 | tf_op jit(solution)/shard_map/while/body/eval_jaxpr/sab,sbc->sac/dot_general | solution.py:30
  848.7 30.7 %select_add_fusion.2 = f32[4,256,768]{2,0,1:T(4,128)S(1)} fusion(f32[4,256,768]{2,0,1:T(4,128)S(1)} %get-tuple-element.206, pred[]{:T(512)S(6)} %compare.49, f32[32,256,768]{2,1,0:T(8,128)} %fusion.29, s32[32]{0:T(128)S(1)} %get-tuple-element.195), kind=kOutput, calls=%fused_computation.11.clone.1 | convolution fusion | flops 303562880 | bytes 31457408 | tf_op jit(solution)/shard_map/while/body/eval_jaxpr/sr,sac->rac/dot_general | solution.py:34
  879.5 2.2 copy.16
  881.7 0.0 all-reduce.5.cloned.1.call-update
  881.7 81.3 %all-reduce.5.cloned.1.call-done = f32[1024,768]{1,0:T(8,128)} async-done(((f32[1024,768]{1,0:T(8,128)}), f32[1024,768]{1,0:T(8,128)}) %all-reduce.5.cloned.1.call-update) | async-done | bytes 3145744 | tf_op jit(solution)/shard_map/psum | solution.py:78
  963.0 3.8 copy.38
  (22 shorter events, 0.2 us)
Async XLA Ops:
  30.4 14.1 %copy-start.4 = (u32[256]{0:T(256)S(1)}, u32[256]{0:T(256)}, u32[]{:S(2)}) copy-start(u32[256]{0:T(256)} %constant.118) | copy-start | bytes 3076
  30.4 15.4 %copy-start.2 = (s32[48]{0:T(128)S(1)}, s32[48]{0:T(128)}, u32[]{:S(2)}) copy-start(s32[48]{0:T(128)} %param.9) | copy-start | bytes 580
  30.4 15.6 %copy-start.3 = (s32[48]{0:T(128)S(1)}, s32[48]{0:T(128)}, u32[]{:S(2)}) copy-start(s32[48]{0:T(128)} %param.8) | copy-start | bytes 580
  30.4 604.5 %copy-start.1 = (s32[256]{0:T(256)S(1)}, s32[256]{0:T(256)}, u32[]{:S(2)}) copy-start(s32[256]{0:T(256)} %param.10) | copy-start | bytes 3076
  30.4 617.5 %all-to-all-start = ((bf16[128,256,256]{2,1,0:T(8,128)(2,1)}), bf16[128,256,256]{2,1,0:T(8,128)(2,1)}, u32[]{:S(2)}, u32[]{:S(2)}) async-start(bf16[128,256,256]{2,1,0:T(8,128)(2,1)} %scatter_fusion.1), calls=%async_computation | async-start | bytes 33554432 | tf_op jit(solution)/shard_map/all_to_all | solution.py:76
  43.6 595.7 %copy-start = (s32[128,2]{1,0:T(8,128)S(1)}, s32[128,2]{1,0:T(8,128)}, u32[]{:S(2)}) copy-start(s32[128,2]{1,0:T(8,128)} %constant.110.clone.1) | copy-start | bytes 3076
  43.6 604.2 %all-gather.2.cloned.1.call-start = ((), (), s32[]{:S(2)}) async-start(), calls=%async_computation.1 | async-start | bytes 7864320 | tf_op jit(solution)/shard_map/all_gather | solution.py:73
  44.4 918.6 %all-reduce.5.cloned.1.call-start = ((), (), s32[]{:S(2)}) async-start(), calls=%async_computation.2 | async-start | bytes 6291456 | tf_op jit(solution)/shard_map/psum | solution.py:78
Sparse Core Ops, SparseCore 0:
  46.3 69.3 all-gather.1
  881.9 81.1 all-reduce.4
where the time goes:
time: 974 us
  blocking collectives  589 us (60%)
  matrix products  194 us (20%)
  waiting for transfers between devices  82 us (8%)
  local copies, waits for them, and re-layouts  78 us (8%)
  between operations  14.2 us (1%)
  starting transfers between devices  13.3 us (1%)
    unnamed x1, blocking collectives  589 us
    dot_general x4, matrix products, one_block(): jnp.einsum('sr,sac->rac', row_hits, products, precision=lax.Precision.HIG...  123 us
    psum x1, waiting for transfers between devices, per_device(): summed = lax.psum(summed, 'grp')  81.3 us
    dot_general x4, matrix products, one_block(): jnp.einsum('sab,sbc->sac', part_tiles, chosen, preferred_element_type=jnp...  70.7 us
    gather x4, local copies, waits for them, and re-layouts, one_block(): chosen = jnp.take(panel_tiles, part_labels[:, 1], axis=0)  37.2 us
  transfers between devices with their start and end apart: 3, of which 1 were waited for; matrix products, arithmetic and copies ran while one was open for 1% of the time, Pallas kernels for 0%

commit v1 on v0

--- a/solution.py
+++ b/solution.py
@@ -1,8 +1,16 @@
+import functools
 import math
 import jax
 import jax.numpy as jnp
 from jax import lax
 from jax.sharding import PartitionSpec as P
+
+
+def step_on_gates(load, group_axis):
+    return lax.all_gather(load, group_axis).sum(axis=0)
+
+
+limits_work = functools.partial(step_on_gates, group_axis="grp")
 
 
 def place_slots(row_ids, owner_map, out_dev):
@@ -75,7 +83,7 @@
     summed = jnp.zeros((out_dev, tile_side, gathered.shape[1]), jnp.float32)
     arrived = lax.all_to_all(outgoing, "wide", split_axis=0, concat_axis=0, tiled=True)
     summed = add_products(summed, arrived, arrived_labels, panel_tiles)
-    summed = lax.psum(summed, "grp")
+    summed = limits_work(summed)
     return summed.reshape(out_dev * tile_side, gathered.shape[1])
 
 

time: 974 us -> 1020 us (1.047)
  waiting for transfers between devices: 82 us -> 122 us
    all_gather x0 -> x1, waiting for transfers between devices: none -> 122 us  [step_on_gates(): return lax.all_gather(load, group_axis).sum(axis=0)]
    psum x1 -> x0, waiting for transfers between devices: 81.3 us -> none  [per_device(): summed = lax.psum(summed, 'grp')]
where the time goes in v1:
time: 1020 us
  blocking collectives  589 us (58%)
  matrix products  194 us (19%)
  waiting for transfers between devices  122 us (12%)
  local copies, waits for them, and re-layouts  74.2 us (7%)
  between operations  14.2 us (1%)
  starting transfers between devices  13.3 us (1%)
  other arithmetic  11.1 us (1%)
    unnamed x1, blocking collectives  589 us
    dot_general x4, matrix products, one_block(): jnp.einsum('sr,sac->rac', row_hits, products, precision=lax.Precision.HIG...  123 us
    all_gather x1, waiting for transfers between devices, step_on_gates(): return lax.all_gather(load, group_axis).sum(axis=0)  122 us
    dot_general x4, matrix products, one_block(): jnp.einsum('sab,sbc->sac', part_tiles, chosen, preferred_element_type=jnp...  70.7 us
    gather x4, local copies, waits for them, and re-layouts, one_block(): chosen = jnp.take(panel_tiles, part_labels[:, 1], axis=0)  37.2 us
  transfers between devices with their start and end apart: 3, of which 1 were waited for; matrix products, arithmetic and copies ran while one was open for 1% of the time, Pallas kernels for 0%

profile of v1, /device:TPU:1, one launch (start us, length us, event | category | flops | bytes accessed | tf_op | source)
XLA Modules:
  0.0 1017.7 jit_solution(15493608791800863690)
XLA Ops:
  6.5 0.9 select_reduce_fusion.1
  7.4 0.2 convert_reduce_fusion.1
  7.6 5.9 broadcast_in_dim.68
  13.5 16.8 %scatter_fusion.1 = bf16[128,256,256]{2,1,0:T(8,128)(2,1)} fusion(bf16[128,256,256]{2,1,0:T(8,128)(2,1)} %broadcast_in_dim.68, s32[48]{0:T(128)S(1)} %fusion.19, bf16[48,256,256]{2,1,0:T(8,128)(2,1)} %param.7), kind=kCustom, calls=%fused_computation.2 | custom fusion | bytes 18874560 | tf_op jit(solution)/shard_map/scatter | solution.py:63
  30.4 0.0 copy-start.4
  30.4 0.0 copy-start.2
  30.4 0.0 copy-start.3
  30.4 0.0 copy-start.1
  30.4 13.3 %all-to-all-start = ((bf16[128,256,256]{2,1,0:T(8,128)(2,1)}), bf16[128,256,256]{2,1,0:T(8,128)(2,1)}, u32[]{:S(2)}, u32[]{:S(2)}) async-start(bf16[128,256,256]{2,1,0:T(8,128)(2,1)} %scatter_fusion.1), calls=%async_computation | async-start | bytes 33554432 | tf_op jit(solution)/shard_map/all_to_all | solution.py:84
  43.6 0.0 copy-start
  43.6 0.0 all-gather.4.cloned.1.call-start
  43.7 0.7 all-gather.4.cloned.1.call-update
  44.4 0.0 all-gather.6.cloned.1.call-start
  44.5 0.0 copy-done.4
  44.5 0.6 dynamic-slice
  45.7 0.0 copy-done.2
  45.7 0.3 dynamic-update-slice
  46.0 0.0 copy-done.3
  46.0 0.3 dynamic-update-slice.1
  46.3 588.5 %all-reduce.2 = (s32[3072]{0:T(1024)S(1)}, s32[3072]{0:T(1024)S(1)}) all-reduce(s32[3072]{0:T(1024)S(1)} %dynamic-update-slice, s32[3072]{0:T(1024)S(1)} %dynamic-update-slice.1), channel_id=1, replica_groups=mesh['grp'=4,'wide'=64] {'wide'}, use_global_device_ids=true, to_apply=%add | all-reduce | flops 6144 | bytes 49152
  634.8 0.1 eq.107
  634.9 0.0 copy-done.1
  634.9 1.7 select_reduce_fusion
  636.6 0.1 reduce_sum.52
  636.7 0.1 copy.20
  636.8 0.5 convert_reduce_fusion
  637.3 0.1 copy.22
  637.4 0.1 add.150
  637.5 0.1 and_select_fusion
  637.6 1.7 copy.23
  639.3 0.0 copy-done
  639.3 8.5 scatter_fusion
  647.8 0.1 copy.24
  647.9 0.0 all-gather.4.cloned.1.call-done
  647.9 0.0 all-to-all-done
  647.9 231.6 %while.14 = (s32[]{:T(128)}, f32[4,256,768]{2,0,1:T(4,128)S(1)}, s32[128,2]{0,1:T(2,128)S(1)}, bf16[128,256,256]{2,1,0:T(8,128)(2,1)}, bf16[16,256,768]{2,1,0:T(...) while((s32[]{:T(128)}, f32[4,256,768]{2,0,1:T(4,128)S(1)}, ...), condition=%wide.region_7.8_spmd.clone, body=%wide.region_6.7_spmd.clone.sunk | while | flops 3531081216 | bytes 98572000 | solution.py:46
  648.1 0.1 constant_dynamic-slice_fusion.2
  648.2 9.4 gather_fusion
  657.5 17.7 %fusion.29 = f32[32,256,768]{2,1,0:T(8,128)} fusion(bf16[32,256,768]{2,1,0:T(8,128)(2,1)} %gather_fusion, pred[32]{0:T(512)(128)(4,1)S(1)} %and_bitcast_fusion.2, bf16[128,256,256]{2,1,0:T(8,128)(2,1)} %get-tuple-element.227, s32[]{:T(128)S(6)} %select_n.171), kind=kOutput, calls=%fused_computation.6.clone.1 | convolution fusion | flops 3227516928 | bytes 41943076 | tf_op jit(solution)/shard_map/while/body/eval_jaxpr/sab,sbc->sac/dot_general | solution.py:38
  675.2 30.7 %select_add_fusion.2 = f32[4,256,768]{2,0,1:T(4,128)S(1)} fusion(f32[4,256,768]{2,0,1:T(4,128)S(1)} %get-tuple-element.216, pred[]{:T(512)S(6)} %compare.49, f32[32,256,768]{2,1,0:T(8,128)} %fusion.29, s32[32]{0:T(128)S(1)} %get-tuple-element.205), kind=kOutput, calls=%fused_computation.11.clone.1 | convolution fusion | flops 303562880 | bytes 31457408 | tf_op jit(solution)/shard_map/while/body/eval_jaxpr/sr,sac->rac/dot_general | solution.py:42
  706.0 0.1 constant_dynamic-slice_fusion.2
  706.1 9.3 gather_fusion
  715.4 17.7 %fusion.29 = f32[32,256,768]{2,1,0:T(8,128)} fusion(bf16[32,256,768]{2,1,0:T(8,128)(2,1)} %gather_fusion, pred[32]{0:T(512)(128)(4,1)S(1)} %and_bitcast_fusion.2, bf16[128,256,256]{2,1,0:T(8,128)(2,1)} %get-tuple-element.227, s32[]{:T(128)S(6)} %select_n.171), kind=kOutput, calls=%fused_computation.6.clone.1 | convolution fusion | flops 3227516928 | bytes 41943076 | tf_op jit(solution)/shard_map/while/body/eval_jaxpr/sab,sbc->sac/dot_general | solution.py:38
  733.1 30.7 %select_add_fusion.2 = f32[4,256,768]{2,0,1:T(4,128)S(1)} fusion(f32[4,256,768]{2,0,1:T(4,128)S(1)} %get-tuple-element.216, pred[]{:T(512)S(6)} %compare.49, f32[32,256,768]{2,1,0:T(8,128)} %fusion.29, s32[32]{0:T(128)S(1)} %get-tuple-element.205), kind=kOutput, calls=%fused_computation.11.clone.1 | convolution fusion | flops 303562880 | bytes 31457408 | tf_op jit(solution)/shard_map/while/body/eval_jaxpr/sr,sac->rac/dot_general | solution.py:42
  763.8 0.1 constant_dynamic-slice_fusion.2
  763.9 9.3 gather_fusion
  773.2 17.7 %fusion.29 = f32[32,256,768]{2,1,0:T(8,128)} fusion(bf16[32,256,768]{2,1,0:T(8,128)(2,1)} %gather_fusion, pred[32]{0:T(512)(128)(4,1)S(1)} %and_bitcast_fusion.2, bf16[128,256,256]{2,1,0:T(8,128)(2,1)} %get-tuple-element.227, s32[]{:T(128)S(6)} %select_n.171), kind=kOutput, calls=%fused_computation.6.clone.1 | convolution fusion | flops 3227516928 | bytes 41943076 | tf_op jit(solution)/shard_map/while/body/eval_jaxpr/sab,sbc->sac/dot_general | solution.py:38
  790.9 30.7 %select_add_fusion.2 = f32[4,256,768]{2,0,1:T(4,128)S(1)} fusion(f32[4,256,768]{2,0,1:T(4,128)S(1)} %get-tuple-element.216, pred[]{:T(512)S(6)} %compare.49, f32[32,256,768]{2,1,0:T(8,128)} %fusion.29, s32[32]{0:T(128)S(1)} %get-tuple-element.205), kind=kOutput, calls=%fused_computation.11.clone.1 | convolution fusion | flops 303562880 | bytes 31457408 | tf_op jit(solution)/shard_map/while/body/eval_jaxpr/sr,sac->rac/dot_general | solution.py:42
  821.7 0.1 constant_dynamic-slice_fusion.2
  821.8 9.2 gather_fusion
  831.0 17.7 %fusion.29 = f32[32,256,768]{2,1,0:T(8,128)} fusion(bf16[32,256,768]{2,1,0:T(8,128)(2,1)} %gather_fusion, pred[32]{0:T(512)(128)(4,1)S(1)} %and_bitcast_fusion.2, bf16[128,256,256]{2,1,0:T(8,128)(2,1)} %get-tuple-element.227, s32[]{:T(128)S(6)} %select_n.171), kind=kOutput, calls=%fused_computation.6.clone.1 | convolution fusion | flops 3227516928 | bytes 41943076 | tf_op jit(solution)/shard_map/while/body/eval_jaxpr/sab,sbc->sac/dot_general | solution.py:38
  848.7 30.7 %select_add_fusion.2 = f32[4,256,768]{2,0,1:T(4,128)S(1)} fusion(f32[4,256,768]{2,0,1:T(4,128)S(1)} %get-tuple-element.216, pred[]{:T(512)S(6)} %compare.49, f32[32,256,768]{2,1,0:T(8,128)} %fusion.29, s32[32]{0:T(128)S(1)} %get-tuple-element.205), kind=kOutput, calls=%fused_computation.11.clone.1 | convolution fusion | flops 303562880 | bytes 31457408 | tf_op jit(solution)/shard_map/while/body/eval_jaxpr/sr,sac->rac/dot_general | solution.py:42
  879.5 2.2 copy.25
  881.7 0.0 all-gather.6.cloned.1.call-update
  881.7 121.5 %all-gather.6.cloned.1.call-done = f32[16,256,768]{2,1,0:T(8,128)} async-done(((f32[4,256,768]{2,1,0:T(8,128)}), f32[16,256,768]{2,1,0:T(8,128)}) %all-gather.6.cloned.1.call-update) | async-done | bytes 12582928 | tf_op jit(solution)/shard_map/all_gather | solution.py:10
  1003.3 7.6 reduce_sum.58
  (22 shorter events, 0.2 us)
Async XLA Ops:
  30.4 14.1 %copy-start.4 = (u32[256]{0:T(256)S(1)}, u32[256]{0:T(256)}, u32[]{:S(2)}) copy-start(u32[256]{0:T(256)} %constant.119) | copy-start | bytes 3076
  30.4 15.4 %copy-start.2 = (s32[48]{0:T(128)S(1)}, s32[48]{0:T(128)}, u32[]{:S(2)}) copy-start(s32[48]{0:T(128)} %param.9) | copy-start | bytes 580
  30.4 15.6 %copy-start.3 = (s32[48]{0:T(128)S(1)}, s32[48]{0:T(128)}, u32[]{:S(2)}) copy-start(s32[48]{0:T(128)} %param.8) | copy-start | bytes 580
  30.4 604.5 %copy-start.1 = (s32[256]{0:T(256)S(1)}, s32[256]{0:T(256)}, u32[]{:S(2)}) copy-start(s32[256]{0:T(256)} %param.10) | copy-start | bytes 3076
  30.4 617.5 %all-to-all-start = ((bf16[128,256,256]{2,1,0:T(8,128)(2,1)}), bf16[128,256,256]{2,1,0:T(8,128)(2,1)}, u32[]{:S(2)}, u32[]{:S(2)}) async-start(bf16[128,256,256]{2,1,0:T(8,128)(2,1)} %scatter_fusion.1), calls=%async_computation | async-start | bytes 33554432 | tf_op jit(solution)/shard_map/all_to_all | solution.py:84
  43.6 595.7 %copy-start = (s32[128,2]{1,0:T(8,128)S(1)}, s32[128,2]{1,0:T(8,128)}, u32[]{:S(2)}) copy-start(s32[128,2]{1,0:T(8,128)} %constant.111.clone.1) | copy-start | bytes 3076
  43.6 604.2 %all-gather.4.cloned.1.call-start = ((), (), s32[]{:S(2)}) async-start(), calls=%async_computation.1 | async-start | bytes 7864320 | tf_op jit(solution)/shard_map/all_gather | solution.py:81
  44.4 958.9 %all-gather.6.cloned.1.call-start = ((), (), s32[]{:S(2)}) async-start(), calls=%async_computation.2 | async-start | bytes 15728640 | tf_op jit(solution)/shard_map/all_gather | solution.py:10
Sparse Core Ops, SparseCore 0:
  46.3 69.3 all-gather.3
  881.9 121.3 all-gather.5
